TPU v7x, 32 devices: a whole 2x2x4 slice. The times are simulated.
32 devices in a mesh: rep: 2 (over y), ctx: 4 (over z), head: 2 (over x), sub: 2 (over core).
Axes of the slice: x: 2, y: 2, z: 4, core: 2. Of those that a mesh axis runs over, the one named last changes fastest.
Arguments:
- hidden_states: bfloat16 [2048, 4096], P(('rep', 'ctx'), ('head', 'sub')), parts along dimension 0, may hold values from -8 to 8
- w_query: bfloat16 [4096, 2048], P('ctx', ('head', 'sub')), may hold values from -0.09375 to 0.09375
- w_key: bfloat16 [4096, 2048], P('ctx', ('head', 'sub')), may hold values from -0.09375 to 0.09375
- w_value: bfloat16 [4096, 2048], P('ctx', ('head', 'sub')), may hold values from -0.09375 to 0.09375
- a_query: bfloat16 [4096, 8], replicated, may hold values from -0.09375 to 0.09375
- a_value: bfloat16 [4096, 8], replicated, may hold values from -0.09375 to 0.09375
- b_query: bfloat16 [8, 2048], P(None, ('head', 'sub')), may hold values from -0.29882812 to 0.29882812
- b_value: bfloat16 [8, 2048], P(None, ('head', 'sub')), may hold values from -0.29882812 to 0.29882812
- positions: int32 [2048], P(('rep', 'ctx')), parts along dimension 0, may hold values from 0 to 99999, as said below
- out_grad: bfloat16 [2048, 2048], P(('rep', 'ctx'), ('head', 'sub')), parts along dimension 0, may hold values from -0.119628906 to 0.119628906
Outputs:
- attn_out: bfloat16 [2048, 2048], P(('rep', 'ctx'), ('head', 'sub')), parts along dimension 0
- grad_a_query: float32 [4096, 16], P(None, 'rep'), parts along dimension 1
- grad_b_query: float32 [16, 2048], P('rep', ('head', 'sub')), parts along dimension 0
- grad_a_value: float32 [4096, 16], P(None, 'rep'), parts along dimension 1
- grad_b_value: float32 [16, 2048], P('rep', ('head', 'sub')), parts along dimension 0
There are 2 independent parts, one for each index of `rep`. A program takes and returns all parts, laid end to end along the dimension named above; an argument that names none is the same for every part. Nothing has to cross between parts.
Inputs may be any that keep to these rules, and one draw needn't show every extreme that they name: `positions`: strictly increasing along the sequence; the first is 0 and the last is 99999.
All inputs are finite; a program needn't handle non-finite values.
Results may differ from a plain program's by a relative error of at most 0.012.
Values may be sent and summed in bfloat16 or wider, within the bound.
A program may use at most 64 MiB of HBM per device.

v0:
```python
import math
import jax
import jax.numpy as jnp
from jax import lax
from jax.sharding import PartitionSpec as P

HEAD_DIM = 128
HEADS = 16
TRAIN_CTX = 4096
MAX_POS = 100000


def passed_along(block, axis, distance):
    devices = range(lax.axis_size(axis))
    route = [((i - distance) % len(devices), i) for i in devices]
    return lax.ppermute(block, axis, route)


def rope_tables(positions):
    half_dim = HEAD_DIM // 2
    inverse = jnp.exp(
        jnp.arange(half_dim, dtype=jnp.float32) * (-2.0 * math.log(10000.0) / HEAD_DIM)
    )
    scaled = positions.astype(jnp.float32) * (TRAIN_CTX / MAX_POS)
    angle = scaled[:, None] * inverse[None, :]
    return (jnp.cos(angle)[:, None, :], jnp.sin(angle)[:, None, :])


def rotate(vectors, cosine, sine):
    half_dim = vectors.shape[-1] // 2
    first = vectors[..., :half_dim]
    second = vectors[..., half_dim:]
    return jnp.concatenate(
        [first * cosine - second * sine, second * cosine + first * sine], axis=-1
    )


def project_back(features, low_grads):
    block_width = min(features.shape[1], 512)
    block_count = features.shape[1] // block_width

    def one_block(number):
        section = lax.dynamic_slice_in_dim(features, number * block_width, block_width, 1).astype(
            jnp.float32
        )
        return lax.dot_general(
            section, low_grads, (((0,), (0,)), ((), ())), precision=lax.Precision.HIGHEST
        )

    blocks = lax.map(one_block, jnp.arange(block_count))
    return blocks.reshape(features.shape[1], low_grads.shape[1])


def local(
    hidden_states, w_query, w_key, w_value, a_query, a_value, b_query, b_value, positions, out_grad
):
    rows_here = hidden_states.shape[0]
    columns = w_query.shape[1]
    heads_here = columns // HEAD_DIM
    rank_cols = a_query.shape[1]
    scale = 1.0 / math.sqrt(HEAD_DIM)
    shard_count = lax.axis_size("ctx")
    total_tokens = rows_here * shard_count
    group_len = total_tokens // 4
    reach = (group_len // 2 % rows_here + group_len - 1) // rows_here
    full_states = lax.all_gather(hidden_states, ("head", "sub"), axis=1, tiled=True)
    pieces = (
        lax.all_gather(w_query, "ctx", axis=0, tiled=True),
        lax.all_gather(w_key, "ctx", axis=0, tiled=True),
        lax.all_gather(w_value, "ctx", axis=0, tiled=True),
    )
    base_q, base_k, base_v = tuple(
        (
            jnp.dot(full_states, weights_piece, preferred_element_type=jnp.float32)
            for weights_piece in pieces
        )
    )
    low_q = jnp.dot(full_states, a_query, preferred_element_type=jnp.float32).astype(jnp.bfloat16)
    low_v = jnp.dot(full_states, a_value, preferred_element_type=jnp.float32).astype(jnp.bfloat16)
    cosine, sine = rope_tables(positions)
    pre_q = base_q + 2.0 * jnp.dot(low_q, b_query, preferred_element_type=jnp.float32)
    queries = rotate(pre_q.reshape(rows_here, heads_here, HEAD_DIM), cosine, sine).astype(
        jnp.bfloat16
    )
    keyed = rotate(base_k.reshape(rows_here, heads_here, HEAD_DIM), cosine, sine).astype(
        jnp.bfloat16
    )
    valued = (base_v + 2.0 * jnp.dot(low_v, b_value, preferred_element_type=jnp.float32)).astype(
        jnp.bfloat16
    )
    valued = valued.reshape(rows_here, heads_here, HEAD_DIM)
    current = jnp.stack([keyed, valued])
    collected = [current]
    for level in range(reach):
        current = passed_along(current, "ctx", 1)
        collected.append(current)
    key_rows = jnp.concatenate([block[0] for block in collected], axis=0)
    value_rows = jnp.concatenate([block[1] for block in collected], axis=0)
    shard_id = lax.axis_index("ctx")
    head_ids = lax.axis_index(("head", "sub")) * heads_here + jnp.arange(heads_here)
    amount = jnp.where(head_ids >= HEADS // 2, group_len // 2, 0).astype(jnp.int32)
    query_pos = shard_id * rows_here + jnp.arange(rows_here, dtype=jnp.int32)
    block_ids = jnp.arange(reach + 1, dtype=jnp.int32)
    source_shard = (shard_id - block_ids) % shard_count
    key_pos = (
        source_shard[:, None] * rows_here + jnp.arange(rows_here, dtype=jnp.int32)[None, :]
    ).reshape(-1)
    query_num = (query_pos[None, :] - amount[:, None]) % total_tokens
    key_num = (key_pos[None, :] - amount[:, None]) % total_tokens
    same_group = key_num[:, None, :] // group_len == query_num[:, :, None] // group_len
    visible = same_group & (key_num[:, None, :] <= query_num[:, :, None])
    scores = (
        jnp.einsum("qhd,khd->hqk", queries, key_rows, preferred_element_type=jnp.float32) * scale
    )
    scores = jnp.where(visible, scores, -jnp.inf)
    highest = jnp.max(scores, axis=-1, keepdims=True)
    expo = jnp.where(visible, jnp.exp(scores - highest), 0.0)
    probs = expo / jnp.sum(expo, axis=-1, keepdims=True)
    probs_b = probs.astype(jnp.bfloat16)
    attended = jnp.einsum("hqk,khd->qhd", probs_b, value_rows, preferred_element_type=jnp.float32)
    attn_out = attended.astype(jnp.bfloat16)
    grads = out_grad.reshape(rows_here, heads_here, HEAD_DIM)
    dprob = jnp.einsum("qhd,khd->hqk", grads, value_rows, preferred_element_type=jnp.float32)
    delta = jnp.sum(grads.astype(jnp.float32) * attn_out.astype(jnp.float32), axis=-1)
    dscore = probs * (dprob - delta.T[:, :, None])
    dscore_b = (dscore * scale).astype(jnp.bfloat16)
    dquery = jnp.einsum("hqk,khd->qhd", dscore_b, key_rows, preferred_element_type=jnp.float32)
    dvalue = jnp.einsum("hqk,qhd->khd", probs_b, grads, preferred_element_type=jnp.float32)
    value_blocks = dvalue.reshape(reach + 1, rows_here, columns)
    carried = value_blocks[reach]
    for level in range(reach, 0, -1):
        carried = passed_along(carried, "ctx", -1) + value_blocks[level - 1]
    dv_local = carried.astype(jnp.bfloat16)
    dq_local = rotate(dquery, cosine, -sine).astype(jnp.bfloat16).reshape(rows_here, columns)
    grad_bq = 2.0 * jnp.dot(low_q.T, dq_local, preferred_element_type=jnp.float32)
    grad_bv = 2.0 * jnp.dot(low_v.T, dv_local, preferred_element_type=jnp.float32)
    low_grads = jnp.concatenate(
        [
            2.0 * jnp.dot(dq_local, b_query.T, preferred_element_type=jnp.float32),
            2.0 * jnp.dot(dv_local, b_value.T, preferred_element_type=jnp.float32),
        ],
        axis=1,
    )
    grad_down = lax.psum(project_back(full_states, low_grads), ("ctx", "head", "sub"))
    grad_bq, grad_bv = lax.psum((grad_bq, grad_bv), "ctx")
    return (
        attn_out.reshape(rows_here, columns),
        grad_down[:, :rank_cols],
        grad_bq,
        grad_down[:, rank_cols:],
        grad_bv,
    )


def solution(mesh):
    in_specs = (
        P(("rep", "ctx"), ("head", "sub")),
        P("ctx", ("head", "sub")),
        P("ctx", ("head", "sub")),
        P("ctx", ("head", "sub")),
        P(),
        P(),
        P(None, ("head", "sub")),
        P(None, ("head", "sub")),
        P(("rep", "ctx")),
        P(("rep", "ctx"), ("head", "sub")),
    )
    out_specs = (
        P(("rep", "ctx"), ("head", "sub")),
        P(None, "rep"),
        P("rep", ("head", "sub")),
        P(None, "rep"),
        P("rep", ("head", "sub")),
    )
    return jax.shard_map(local, mesh=mesh, in_specs=in_specs, out_specs=out_specs, check_vma=False)
```

profile of v0, /device:TPU:0, one launch (start us, length us, event | category | flops | bytes accessed | tf_op | source)
XLA Modules:
  0.0 444.1 jit_solution(10380813642152723503)
XLA Ops:
  7.2 0.7 all-gather.5.cloned.1.call-update
  8.0 0.7 all-gather.9.cloned.1.call-update
  8.7 0.7 all-gather.11.cloned.1.call-update
  9.5 0.5 all-gather.7.cloned.1.call-update
  10.2 1.3 fusion.23
  11.5 23.4 %all-gather.5.cloned.1.call-done = bf16[256,4096]{1,0:T(8,128)(2,1)} async-done(((bf16[256,1024]{1,0:T(8,128)(2,1)}), bf16[256,4096]{1,0:T(8,128)(2,1)}) %all-gather.5.cloned.1.call-update) | async-done | bytes 2097168 | tf_op jit(solution)/shard_map/all_gather | solution.py:66
  34.9 2.4 convolution_convert_fusion.1
  37.3 0.7 convolution_convert_fusion.2
  38.0 79.3 %all-gather.9.cloned.1.call-done = bf16[4096,512]{1,0:T(8,128)(2,1)} async-done(((bf16[1024,512]{1,0:T(8,128)(2,1)}), bf16[4096,512]{1,0:T(8,128)(2,1)}) %all-gather.9.cloned.1.call-update) | async-done | bytes 4194320 | tf_op jit(solution)/shard_map/all_gather | solution.py:69
  117.2 3.4 fusion.50
  120.7 0.2 reshape.368
  120.9 77.2 %all-gather.11.cloned.1.call-done = bf16[4096,512]{1,0:T(8,128)(2,1)} async-done(((bf16[1024,512]{1,0:T(8,128)(2,1)}), bf16[4096,512]{1,0:T(8,128)(2,1)}) %all-gather.11.cloned.1.call-update) | async-done | bytes 4194320 | tf_op jit(solution)/shard_map/all_gather | solution.py:68
  198.1 3.4 fusion.51
  201.5 1.1 fusion.9
  202.6 1.2 reshape.369
  203.8 74.9 %all-gather.7.cloned.1.call-done = bf16[4096,512]{1,0:T(8,128)(2,1)} async-done(((bf16[1024,512]{1,0:T(8,128)(2,1)}), bf16[4096,512]{1,0:T(8,128)(2,1)}) %all-gather.7.cloned.1.call-update) | async-done | bytes 4194320 | tf_op jit(solution)/shard_map/all_gather | solution.py:70
  278.8 3.4 fusion.49
  282.2 0.3 fusion.10
  282.5 0.8 stack_reshape.3
  283.2 1.0 copy.29
  284.3 0.6 fusion.45
  284.9 0.3 copy-done.2
  285.2 1.1 subtract_convert_fusion.1
  286.3 1.0 pad_maximum_fusion
  287.4 1.8 copy.34
  289.2 0.8 copy_bitcast_fusion
  290.0 12.8 %collective-permute-done = bf16[2,256,4,128]{3,1,2,0:T(8,128)(2,1)S(1)} collective-permute-done((bf16[2,256,4,128]{3,1,2,0:T(8,128)(2,1)}, bf16[2,256,4,128]{3,1,2,0:T(8,128)(2,1)S(1)}, u32[]{:S(2)}, u32[]{:S(2)}) %collective-permute-start) | collective-permute-done | bytes 524320 | tf_op jit(solution)/shard_map/ppermute | solution.py:16
  302.8 0.8 slice_bitcast_fusion
  303.6 4.7 %fusion.48 = (f32[4,256]{1,0:T(4,128)S(1)}, f32[4,256,512]{2,1,0:T(8,128)}) fusion(s32[4,256]{1,0:T(4,128)S(1)} %get-tuple-element.79, s32[4,512]{1,0:T(4,128)S(1)} %get-tuple-element.74, s32[4,256]{1,0:T(4,128)S(1)} %get-tuple-element.78, s32[4,512]{1,0:T(4,128)S(1)} %get-tuple-element.73, bf16[256,4,64]{2,0,1:T(8,128)(2,1)} %get-tuple-element.56, ...), kind=kOutput, calls=%fused_computation.106 | convolution fusion | flops 142082560 | bytes 2912256 | tf_op jit(solution)/shard_map/sub | solution.py:117
  308.4 3.1 convolution_bitcast_fusion.1
  311.5 1.3 multiply_reduce_fusion
  312.9 2.6 fusion.7
  315.5 2.2 fusion.44
  317.7 0.3 subtract_convert_fusion
  318.0 0.1 pad_maximum_fusion.7
  318.3 1.8 copy.39
  320.2 0.2 convolution_multiply_fusion.3
  320.4 10.3 %collective-permute-done.1 = f32[256,512]{0,1:T(8,128)} collective-permute-done((f32[256,512]{0,1:T(8,128)}, f32[256,512]{0,1:T(8,128)}, u32[]{:S(2)}, u32[]{:S(2)}) %collective-permute-start.1) | collective-permute-done | bytes 524320 | tf_op jit(solution)/shard_map/ppermute | solution.py:16
  330.7 1.1 fusion.20
  332.0 13.4 %while.10 = (s32[]{:T(128)}, f32[8,512,16]{1,0,2:T(8,128)S(1)}, s32[8]{0:T(128)S(1)}, bf16[256,4096]{1,0:T(8,128)(2,1)S(1)}, f32[256,16]{0,1:T(8,128)S(1)}, /*index=5*/s32[]{:T(128)}, s32[1]{0:T(128)}, s32[]{:T(128)}, s32[]{:T(128)}) while((s32[]{:T(128)}, f32[8,512,16]{1,0,2:T(8,128)S(1)}, s32[8]{0:T(128)S(1)}, ...), condition=%wide.region_4.5_spmd, body=%wide.region_3.4_spmd.sunk | while | flops 25165828 | bytes 442535 | solution.py:50
  332.0 0.6 dynamic_slice.12
  333.2 0.2 convolution_bitcast_fusion.3
  333.6 0.6 dynamic_slice.12
  334.9 0.2 convolution_bitcast_fusion.3
  335.3 0.6 dynamic_slice.12
  336.6 0.2 convolution_bitcast_fusion.3
  337.0 0.6 dynamic_slice.12
  338.2 0.2 convolution_bitcast_fusion.3
  338.5 0.1 dynamic_update_slice.5
  338.7 0.6 dynamic_slice.12
  339.9 0.2 convolution_bitcast_fusion.3
  340.4 0.6 dynamic_slice.12
  341.6 0.2 convolution_bitcast_fusion.3
  341.9 0.1 dynamic_update_slice.5
  342.0 0.6 dynamic_slice.12
  343.3 0.2 convolution_bitcast_fusion.3
  343.7 0.6 dynamic_slice.12
  344.9 0.2 convolution_bitcast_fusion.3
  345.2 0.1 dynamic_update_slice.5
  345.4 0.9 copy.53
  346.3 0.2 convolution_multiply_fusion.2
  346.4 18.4 %all-reduce = (f32[8,512]{1,0:T(8,128)}, f32[8,512]{1,0:T(8,128)}) all-reduce(f32[8,512]{1,0:T(8,128)S(1)} %convolution_multiply_fusion.3, f32[8,512]{1,0:T(8,128)S(1)} %convolution_multiply_fusion.2), channel_id=1, replica_groups=mesh['rep'=2,'ctx'=4,'head'=2,'sub'=2] {'ctx'}, use_global_device_ids=true, to_apply=%region_6.7 | all-reduce | flops 8192 | bytes 65536 | tf_op jit(solution)/shard_map/psum | solution.py:145
  364.8 71.1 %all-reduce.3.cloned.1.call-done = f32[4096,16]{0,1:T(8,128)} async-done(((f32[4096,16]{0,1:T(8,128)}), f32[4096,16]{0,1:T(8,128)}) %all-reduce.3.cloned.1.call-update) | async-done | bytes 262160 | tf_op jit(solution)/shard_map/psum | solution.py:144
  435.9 1.7 fusion.47
  (65 shorter events, 2.1 us)
Async XLA Ops:
  7.2 27.7 %copy-start = (bf16[4096,8]{0,1:T(8,128)(2,1)S(1)}, bf16[4096,8]{0,1:T(8,128)(2,1)}, u32[]{:S(2)}) copy-start(bf16[4096,8]{0,1:T(8,128)(2,1)} %param.16) | copy-start | bytes 196612
  7.2 2.9 copy-start.13
  7.2 27.7 %all-gather.5.cloned.1.call-start = ((), (), s32[]{:S(2)}) async-start(), calls=%async_computation | async-start | bytes 2621440 | tf_op jit(solution)/shard_map/all_gather | solution.py:66
  7.9 109.3 %all-gather.9.cloned.1.call-start = ((), (), s32[]{:S(2)}) async-start(), calls=%async_computation.2 | async-start | bytes 5242880 | tf_op jit(solution)/shard_map/all_gather | solution.py:69
  8.7 28.6 %copy-start.10 = (bf16[4096,8]{0,1:T(8,128)(2,1)S(1)}, bf16[4096,8]{0,1:T(8,128)(2,1)}, u32[]{:S(2)}) copy-start(bf16[4096,8]{0,1:T(8,128)(2,1)} %param.17) | copy-start | bytes 196612
  8.7 189.4 %all-gather.11.cloned.1.call-start = ((), (), s32[]{:S(2)}) async-start(), calls=%async_computation.3 | async-start | bytes 5242880 | tf_op jit(solution)/shard_map/all_gather | solution.py:68
  9.4 269.3 %all-gather.7.cloned.1.call-start = ((), (), s32[]{:S(2)}) async-start(), calls=%async_computation.1 | async-start | bytes 5242880 | tf_op jit(solution)/shard_map/all_gather | solution.py:70
  10.0 425.9 %all-reduce.3.cloned.1.call-start = ((), (), s32[]{:S(2)}) async-start(), calls=%async_computation.4 | async-start | bytes 524288 | tf_op jit(solution)/shard_map/psum | solution.py:144
  34.9 2.4 copy-start.1
  120.9 80.7 %copy-start.11 = (bf16[8,512]{1,0:T(8,128)(2,1)S(1)}, bf16[8,512]{1,0:T(8,128)(2,1)}, u32[]{:S(2)}) copy-start(bf16[8,512]{1,0:T(8,128)(2,1)} %param.18) | copy-start | bytes 24580
  203.8 78.4 %copy-start.12 = (bf16[8,512]{1,0:T(8,128)(2,1)S(1)}, bf16[8,512]{1,0:T(8,128)(2,1)}, u32[]{:S(2)}) copy-start(bf16[8,512]{1,0:T(8,128)(2,1)} %param.19) | copy-start | bytes 24580
  284.2 0.9 copy-start.2
  284.2 1.0 copy-start.5
  287.3 15.5 %collective-permute-start = (bf16[2,256,4,128]{3,1,2,0:T(8,128)(2,1)}, bf16[2,256,4,128]{3,1,2,0:T(8,128)(2,1)S(1)}, u32[]{:S(2)}, u32[]{:S(2)}) collective-permute-start(bf16[2,256,4,128]{3,1,2,0:T(8,128)(2,1)} %pad_maximum_fusion), channel_id=1, source_target_pairs={{12,0},{0,4},{4,8},{8,12},{13,1},{1,5},{5,9},{9,13},{14,2},{2,6},{... | collective-permute-start | bytes 1572872 | tf_op jit(solution)/shard_map/ppermute | solution.py:16
  303.6 4.8 %copy-start.7 = (bf16[256,512]{0,1:T(8,128)(2,1)S(1)}, bf16[256,512]{0,1:T(8,128)(2,1)}, u32[]{:S(2)}) copy-start(bf16[256,512]{0,1:T(8,128)(2,1)} %copy.34) | copy-start | bytes 786436
  308.4 3.1 copy-start.8
  308.4 3.1 copy-start.9
  308.4 3.1 copy-start.14
  315.5 2.2 copy-start.3
  315.5 2.2 copy-start.4
  317.7 13.0 %collective-permute-start.1 = (f32[256,512]{0,1:T(8,128)}, f32[256,512]{0,1:T(8,128)}, u32[]{:S(2)}, u32[]{:S(2)}) collective-permute-start(f32[256,512]{0,1:T(8,128)} %bitcast.14), channel_id=1, source_target_pairs={{4,0},{8,4},{12,8},{0,12},{5,1},{9,5},{13,9},{1,13},{6,2},{10,6},{... | collective-permute-start | bytes 1572872 | tf_op jit(solution)/shard_map/ppermute | solution.py:16
  318.0 14.0 %copy-start.6 = (f32[8,512,16]{1,0,2:T(8,128)S(1)}, f32[8,512,16]{1,0,2:T(8,128)}, u32[]{:S(2)}) copy-start(f32[8,512,16]{1,0,2:T(8,128)} %custom-call) | copy-start | bytes 786436
Sparse Core Ops, SparseCore 0:
  9.6 25.2 all-gather.4
  36.5 80.7 all-gather.8
  118.8 79.2 all-gather.10
  199.5 79.2 all-gather.6
  346.4 89.4 all-reduce.2
where the time goes:
time: 445 us; the launch traced here: 444 us
  waiting for transfers between devices  352 us (79%)
  matrix products  28.9 us (6%)
  local copies, waits for them, and re-layouts  20.4 us (5%)
  blocking collectives  18.4 us (4%)
  between operations  14.1 us (3%)
  loops' own time  5.47 us (1%)
  other arithmetic  5.13 us (1%)
    all_gather x1, waiting for transfers between devices, local(): lax.all_gather(w_key, 'ctx', axis=0, tiled=True)  79.3 us
    all_gather x1, waiting for transfers between devices, local(): lax.all_gather(w_query, 'ctx', axis=0, tiled=True)  77.2 us
    all_gather x1, waiting for transfers between devices, local(): lax.all_gather(w_value, 'ctx', axis=0, tiled=True)  74.9 us
    psum x1, waiting for transfers between devices, local(): lax.psum(project_back(full_states, low_grads), ('ctx', 'head', 'sub'))  71.1 us
    all_gather x1, waiting for transfers between devices, local(): lax.all_gather(hidden_states, ('head', 'sub'), axis=1, tiled=True)  23.4 us
    ppermute x2, waiting for transfers between devices, passed_along(): return lax.ppermute(block, axis, route)  23.1 us
    psum x1, blocking collectives, local(): grad_bq, grad_bv = lax.psum((grad_bq, grad_bv), 'ctx')  18.4 us
    dot_general x3, matrix products, local(): jnp.dot(full_states, weights_piece, preferred_element_type=jnp.float32)  10.3 us
  transfers between devices with their start and end apart: 7, of which 7 were waited for; matrix products, arithmetic and copies ran while one was open for 4% of the time, Pallas kernels for 0%

commit v1 on v0

--- a/solution.py
+++ b/solution.py
@@ -141,7 +141,9 @@
         ],
         axis=1,
     )
-    grad_down = lax.psum(project_back(full_states, low_grads), ("ctx", "head", "sub"))
+    grad_down = jnp.sum(
+        lax.all_gather(project_back(full_states, low_grads), ("ctx", "head", "sub")), axis=0
+    )
     grad_bq, grad_bv = lax.psum((grad_bq, grad_bv), "ctx")
     return (
         attn_out.reshape(rows_here, columns),

time: 445 us -> 422 us (0.948)
  waiting for transfers between devices: 352 us -> 315 us
  local copies, waits for them, and re-layouts: 20.4 us -> 30.7 us
    psum x1 -> x0, waiting for transfers between devices: 71.1 us -> none  [local(): lax.psum(project_back(full_states, low_grads), ('ctx', 'head', 'sub'))]
    all_gather x0 -> x1, waiting for transfers between devices: none -> 30.5 us  [local(): lax.all_gather(project_back(full_states, low_grads), ('ctx', 'head', 'sub'))]
    dynamic_update_slice x16, local copies, waits for them, and re-layouts: 1.47 us -> 14.3 us  [project_back(): blocks = lax.map(one_block, jnp.arange(block_count))]
where the time goes in v1:
time: 422 us; the launch traced here: 421 us
  waiting for transfers between devices  315 us (75%)
  local copies, waits for them, and re-layouts  30.7 us (7%)
  matrix products  29.3 us (7%)
  blocking collectives  18.9 us (4%)
  between operations  14.1 us (3%)
  other arithmetic  7.52 us (2%)
  loops' own time  5.32 us (1%)
    all_gather x1, waiting for transfers between devices, local(): lax.all_gather(w_key, 'ctx', axis=0, tiled=True)  79.3 us
    all_gather x1, waiting for transfers between devices, local(): lax.all_gather(w_query, 'ctx', axis=0, tiled=True)  77.2 us
    all_gather x1, waiting for transfers between devices, local(): lax.all_gather(w_value, 'ctx', axis=0, tiled=True)  74.9 us
    all_gather x1, waiting for transfers between devices, local(): lax.all_gather(project_back(full_states, low_grads), ('ctx', 'head', 'sub'))  30.5 us
    ppermute x2, waiting for transfers between devices, passed_along(): return lax.ppermute(block, axis, route)  27.5 us
    all_gather x1, waiting for transfers between devices, local(): lax.all_gather(hidden_states, ('head', 'sub'), axis=1, tiled=True)  23.4 us
    psum x1, blocking collectives, local(): grad_bq, grad_bv = lax.psum((grad_bq, grad_bv), 'ctx')  18.9 us
    dynamic_update_slice x16, local copies, waits for them, and re-layouts, project_back(): blocks = lax.map(one_block, jnp.arange(block_count))  14.3 us
  transfers between devices with their start and end apart: 7, of which 7 were waited for; matrix products, arithmetic and copies ran while one was open for 4% of the time, Pallas kernels for 0%

profile of v1, /device:TPU:0, one launch (start us, length us, event | category | flops | bytes accessed | tf_op | source)
XLA Modules:
  0.0 421.3 jit_solution(10711146232651518942)
XLA Ops:
  7.2 0.7 all-gather.6.cloned.1.call-update
  8.0 0.7 all-gather.10.cloned.1.call-update
  8.7 0.7 all-gather.12.cloned.1.call-update
  9.5 0.5 all-gather.8.cloned.1.call-update
  10.2 1.3 fusion.23
  11.5 23.4 %all-gather.6.cloned.1.call-done = bf16[256,4096]{1,0:T(8,128)(2,1)} async-done(((bf16[256,1024]{1,0:T(8,128)(2,1)}), bf16[256,4096]{1,0:T(8,128)(2,1)}) %all-gather.6.cloned.1.call-update) | async-done | bytes 2097168 | tf_op jit(solution)/shard_map/all_gather | solution.py:66
  34.9 2.4 convolution_convert_fusion.1
  37.3 0.7 convolution_convert_fusion.2
  38.0 79.3 %all-gather.10.cloned.1.call-done = bf16[4096,512]{1,0:T(8,128)(2,1)} async-done(((bf16[1024,512]{1,0:T(8,128)(2,1)}), bf16[4096,512]{1,0:T(8,128)(2,1)}) %all-gather.10.cloned.1.call-update) | async-done | bytes 4194320 | tf_op jit(solution)/shard_map/all_gather | solution.py:69
  117.2 3.4 fusion.50
  120.9 77.2 %all-gather.12.cloned.1.call-done = bf16[4096,512]{1,0:T(8,128)(2,1)} async-done(((bf16[1024,512]{1,0:T(8,128)(2,1)}), bf16[4096,512]{1,0:T(8,128)(2,1)}) %all-gather.12.cloned.1.call-update) | async-done | bytes 4194320 | tf_op jit(solution)/shard_map/all_gather | solution.py:68
  198.1 3.4 fusion.51
  201.5 1.1 fusion.9
  202.6 1.2 reshape.366
  203.8 74.9 %all-gather.8.cloned.1.call-done = bf16[4096,512]{1,0:T(8,128)(2,1)} async-done(((bf16[1024,512]{1,0:T(8,128)(2,1)}), bf16[4096,512]{1,0:T(8,128)(2,1)}) %all-gather.8.cloned.1.call-update) | async-done | bytes 4194320 | tf_op jit(solution)/shard_map/all_gather | solution.py:70
  278.7 3.4 fusion.49
  282.2 0.3 fusion.10
  282.5 0.8 stack_reshape.3
  283.2 1.0 copy.41
  284.3 0.6 fusion.45
  284.9 0.3 copy-done.2
  285.2 1.1 subtract_convert_fusion.1
  286.3 1.0 pad_maximum_fusion
  287.7 15.2 %collective-permute-done = bf16[2,256,4,128]{3,1,2,0:T(8,128)(2,1)} collective-permute-done((bf16[2,256,4,128]{3,1,2,0:T(8,128)(2,1)}, bf16[2,256,4,128]{3,1,2,0:T(8,128)(2,1)}, u32[]{:S(2)}, u32[]{:S(2)}) %collective-permute-start) | collective-permute-done | bytes 524320 | tf_op jit(solution)/shard_map/ppermute | solution.py:16
  302.9 1.8 slice_bitcast_fusion
  304.7 4.7 %fusion.48 = (f32[4,256]{1,0:T(4,128)S(1)}, f32[4,256,512]{2,1,0:T(8,128)}) fusion(s32[4,256]{1,0:T(4,128)S(1)} %get-tuple-element.84, s32[4,512]{1,0:T(4,128)S(1)} %get-tuple-element.79, s32[4,256]{1,0:T(4,128)S(1)} %get-tuple-element.83, s32[4,512]{1,0:T(4,128)S(1)} %get-tuple-element.78, bf16[256,4,64]{2,0,1:T(8,128)(2,1)} %get-tuple-element.61, ...), kind=kOutput, calls=%fused_computation.106 | convolution fusion | flops 142082560 | bytes 2912256 | tf_op jit(solution)/shard_map/sub | solution.py:117
  309.4 3.1 convolution_bitcast_fusion.1
  312.6 1.6 multiply_reduce_fusion
  314.2 2.7 fusion.7
  316.9 2.2 fusion.44
  319.1 0.3 subtract_convert_fusion
  319.8 12.3 %collective-permute-done.1 = f32[256,512]{0,1:T(8,128)} collective-permute-done((f32[256,512]{0,1:T(8,128)}, f32[256,512]{0,1:T(8,128)}, u32[]{:S(2)}, u32[]{:S(2)}) %collective-permute-start.1) | collective-permute-done | bytes 524320 | tf_op jit(solution)/shard_map/ppermute | solution.py:16
  332.1 1.1 fusion.20
  333.3 26.1 %while.10 = (s32[]{:T(128)}, f32[8,512,16]{1,0,2:T(8,128)}, s32[8]{0:T(128)S(1)}, bf16[256,4096]{1,0:T(8,128)(2,1)S(1)}, f32[256,16]{0,1:T(8,128)S(1)}, /*index=5*/s32[]{:T(128)}, s32[1]{0:T(128)}, s32[]{:T(128)}, s32[]{:T(128)}) while((s32[]{:T(128)}, f32[8,512,16]{1,0,2:T(8,128)}, s32[8]{0:T(128)S(1)}, bf16[256,4096]{1,0:T(8,128)(2,1)S(1)}, ...), condition=%wide.region_4.5_spmd, body=%wide.region_3.4_spmd.sunk | while | flops 25165828 | bytes 442535 | solution.py:50
  333.3 0.6 dynamic_slice.12
  334.6 0.2 convolution_bitcast_fusion.3
  334.8 1.8 dynamic_update_slice.5
  336.6 0.6 dynamic_slice.12
  337.8 0.2 convolution_bitcast_fusion.3
  338.1 1.8 dynamic_update_slice.5
  339.9 0.6 dynamic_slice.12
  341.1 0.2 convolution_bitcast_fusion.3
  341.4 1.8 dynamic_update_slice.5
  343.1 0.6 dynamic_slice.12
  344.4 0.2 convolution_bitcast_fusion.3
  344.6 1.8 dynamic_update_slice.5
  346.4 0.6 dynamic_slice.12
  347.6 0.2 convolution_bitcast_fusion.3
  347.9 1.8 dynamic_update_slice.5
  349.6 0.6 dynamic_slice.12
  350.9 0.2 convolution_bitcast_fusion.3
  351.1 1.8 dynamic_update_slice.5
  352.9 0.6 dynamic_slice.12
  354.1 0.2 convolution_bitcast_fusion.3
  354.4 1.8 dynamic_update_slice.5
  356.1 0.6 dynamic_slice.12
  357.4 0.2 convolution_bitcast_fusion.3
  357.6 1.8 dynamic_update_slice.5
  359.4 1.7 all_gather_reshape.3
  361.1 0.8 copy.53
  362.3 18.9 %all-reduce = (f32[8,512]{1,0:T(8,128)}, f32[8,512]{1,0:T(8,128)}) all-reduce(f32[8,512]{1,0:T(8,128)S(1)} %convolution_multiply_fusion.3, f32[8,512]{1,0:T(8,128)S(1)} %convolution_multiply_fusion.2), channel_id=1, replica_groups=mesh['rep'=2,'ctx'=4,'head'=2,'sub'=2] {'ctx'}, use_global_device_ids=true, to_apply=%region_6.7 | all-reduce | flops 8192 | bytes 65536 | tf_op jit(solution)/shard_map/psum | solution.py:147
  381.2 30.5 %all-gather.14.cloned.1.call-done = f32[16,4096,16]{1,2,0:T(8,128)} async-done(((f32[1,4096,16]{1,2,0:T(8,128)}), f32[16,4096,16]{1,2,0:T(8,128)}) %all-gather.14.cloned.1.call-update) | async-done | bytes 4194320 | tf_op jit(solution)/shard_map/all_gather | solution.py:145
  411.7 2.4 reduce_sum.29
  414.1 0.7 fusion.47
  (68 shorter events, 2.2 us)
Async XLA Ops:
  7.2 27.7 %copy-start = (bf16[4096,8]{0,1:T(8,128)(2,1)S(1)}, bf16[4096,8]{0,1:T(8,128)(2,1)}, u32[]{:S(2)}) copy-start(bf16[4096,8]{0,1:T(8,128)(2,1)} %param.16) | copy-start | bytes 196612
  7.2 2.9 copy-start.14
  7.2 27.7 %all-gather.6.cloned.1.call-start = ((), (), s32[]{:S(2)}) async-start(), calls=%async_computation | async-start | bytes 2621440 | tf_op jit(solution)/shard_map/all_gather | solution.py:66
  7.9 109.3 %all-gather.10.cloned.1.call-start = ((), (), s32[]{:S(2)}) async-start(), calls=%async_computation.2 | async-start | bytes 5242880 | tf_op jit(solution)/shard_map/all_gather | solution.py:69
  8.7 28.6 %copy-start.11 = (bf16[4096,8]{0,1:T(8,128)(2,1)S(1)}, bf16[4096,8]{0,1:T(8,128)(2,1)}, u32[]{:S(2)}) copy-start(bf16[4096,8]{0,1:T(8,128)(2,1)} %param.17) | copy-start | bytes 196612
  8.7 189.4 %all-gather.12.cloned.1.call-start = ((), (), s32[]{:S(2)}) async-start(), calls=%async_computation.3 | async-start | bytes 5242880 | tf_op jit(solution)/shard_map/all_gather | solution.py:68
  9.4 269.3 %all-gather.8.cloned.1.call-start = ((), (), s32[]{:S(2)}) async-start(), calls=%async_computation.1 | async-start | bytes 5242880 | tf_op jit(solution)/shard_map/all_gather | solution.py:70
  10.0 401.7 %all-gather.14.cloned.1.call-start = ((), (), s32[]{:S(2)}) async-start(), calls=%async_computation.4 | async-start | bytes 4456448 | tf_op jit(solution)/shard_map/all_gather | solution.py:145
  34.9 2.4 copy-start.1
  120.9 80.6 %copy-start.12 = (bf16[8,512]{1,0:T(8,128)(2,1)S(1)}, bf16[8,512]{1,0:T(8,128)(2,1)}, u32[]{:S(2)}) copy-start(bf16[8,512]{1,0:T(8,128)(2,1)} %param.18) | copy-start | bytes 24580
  203.8 78.4 %copy-start.13 = (bf16[8,512]{1,0:T(8,128)(2,1)S(1)}, bf16[8,512]{1,0:T(8,128)(2,1)}, u32[]{:S(2)}) copy-start(bf16[8,512]{1,0:T(8,128)(2,1)} %param.19) | copy-start | bytes 24580
  284.2 0.9 copy-start.2
  284.2 1.0 copy-start.5
  285.2 2.1 copy-start.6
  287.3 15.6 %collective-permute-start = (bf16[2,256,4,128]{3,1,2,0:T(8,128)(2,1)}, bf16[2,256,4,128]{3,1,2,0:T(8,128)(2,1)}, u32[]{:S(2)}, u32[]{:S(2)}) collective-permute-start(bf16[2,256,4,128]{3,1,2,0:T(8,128)(2,1)} %pad_maximum_fusion), channel_id=1, source_target_pairs={{12,0},{0,4},{4,8},{8,12},{13,1},{1,5},{5,9},{9,13},{14,2},{2,6},{... | collective-permute-start | bytes 1572872 | tf_op jit(solution)/shard_map/ppermute | solution.py:16
  287.5 21.9 %copy-start.7 = (bf16[256,512]{0,1:T(8,128)(2,1)}, bf16[256,512]{0,1:T(8,128)(2,1)S(1)}, u32[]{:S(2)}) copy-start(bf16[256,512]{0,1:T(8,128)(2,1)S(1)} %copy.46) | copy-start | bytes 786436
  287.6 24.9 %copy-start.8 = (bf16[256,4,128]{2,0,1:T(8,128)(2,1)}, bf16[256,4,128]{2,0,1:T(8,128)(2,1)S(1)}, u32[]{:S(2)}) copy-start(bf16[256,4,128]{2,0,1:T(8,128)(2,1)S(1)} %copy_bitcast_fusion) | copy-start | bytes 786436
  304.7 4.7 %copy-start.9 = (bf16[256,4,128]{2,0,1:T(8,128)(2,1)}, bf16[256,4,128]{2,0,1:T(8,128)(2,1)S(1)}, u32[]{:S(2)}) copy-start(bf16[256,4,128]{2,0,1:T(8,128)(2,1)S(1)} %get-tuple-element.68) | copy-start | bytes 786436
  309.4 3.2 copy-start.10
  309.4 3.1 copy-start.15
  316.9 2.2 copy-start.3
  316.9 2.2 copy-start.4
  319.1 13.0 %collective-permute-start.1 = (f32[256,512]{0,1:T(8,128)}, f32[256,512]{0,1:T(8,128)}, u32[]{:S(2)}, u32[]{:S(2)}) collective-permute-start(f32[256,512]{0,1:T(8,128)} %bitcast.14), channel_id=1, source_target_pairs={{4,0},{8,4},{12,8},{0,12},{5,1},{9,5},{13,9},{1,13},{6,2},{10,6},{... | collective-permute-start | bytes 1572872 | tf_op jit(solution)/shard_map/ppermute | solution.py:16
Sparse Core Ops, SparseCore 0:
  9.6 25.2 all-gather.5
  36.5 80.7 all-gather.9
  118.8 79.2 all-gather.11
  199.5 79.2 all-gather.7
  361.3 50.3 all-gather.13
